TPU v7x, 32 devices: a whole 2x2x4 slice. The times are simulated.
32 devices in a mesh: groups: 2 (over y), lon: 4 (over z), lat: 2 (over x), head: 2 (over core).
Axes of the slice: x: 2, y: 2, z: 4, core: 2. Of those that a mesh axis runs over, the one named last changes fastest.
Arguments:
- queries: bfloat16 [4, 4, 128, 1536], P(('groups', 'lat'), 'lon', None, 'head'), parts along dimension 0, may hold values from -12 to 12
- key_tokens: bfloat16 [4, 4, 128, 1536], P(('groups', 'lat'), 'lon', None, 'head'), parts along dimension 0, may hold values from -4 to 4
- value_tokens: bfloat16 [4, 4, 128, 1536], P(('groups', 'lat'), 'lon', None, 'head'), parts along dimension 0, may hold values from -6 to 6
- out_grad: bfloat16 [4, 4, 128, 1536], P(('groups', 'lat'), 'lon', None, 'head'), parts along dimension 0, may hold values from -6 to 6
- counts: int32 [4, 4], P('groups'), parts along dimension 0, may hold values from 16 to 128, as said below
Outputs:
- attended: bfloat16 [4, 4, 128, 1536], P(('groups', 'lat'), 'lon', None, 'head'), parts along dimension 0
- query_grad: bfloat16 [4, 4, 128, 1536], P(('groups', 'lat'), 'lon', None, 'head'), parts along dimension 0
- key_grad: bfloat16 [4, 4, 128, 1536], P(('groups', 'lat'), 'lon', None, 'head'), parts along dimension 0
- value_grad: bfloat16 [4, 4, 128, 1536], P(('groups', 'lat'), 'lon', None, 'head'), parts along dimension 0
There are 2 independent parts, one for each index of `groups`. A program takes and returns all parts, laid end to end along the dimension named above; each array names one. Nothing has to cross between parts.
Inputs may be any that keep to these rules, and one draw needn't show every extreme that they name: `counts`: every row of tiles holds a tile of 128 valid tokens; tiles of the first and last rows hold at least 16 valid tokens, the others at least 64.
All inputs are finite; a program needn't handle non-finite values.
Results may differ from a plain program's by a relative error of at most 0.012.
The roundings to bfloat16 on the way count: a program that leaves them out, or rounds other values in their place, can miss the bound.
Values may be sent and summed in bfloat16 or wider, within the bound.
A program may use at most 64 MiB of HBM per device.

v0:
```python
import math

import jax
import jax.numpy as jnp
from jax import lax
from jax.sharding import PartitionSpec as P

HD = 128


def with_halo(cells, sides, width, closed):
    for axis, dim in sides:
        count = lax.axis_size(axis)
        ends = count if closed else count - 1
        head = lax.slice_in_dim(cells, 0, width, axis=dim)
        tail = lax.slice_in_dim(cells, cells.shape[dim] - width, cells.shape[dim], axis=dim)
        cells = jnp.concatenate(
            [
                lax.ppermute(tail, axis, [(i, (i + 1) % count) for i in range(ends)]),
                cells,
                lax.ppermute(head, axis, [((i + 1) % count, i) for i in range(ends)]),
            ],
            axis=dim,
        )
    return cells


def passed_along(block, axis, distance):
    devices = range(lax.axis_size(axis))
    route = [((i - distance) % len(devices), i) for i in devices]
    return lax.ppermute(block, axis, route)


def neighbour_tiles(row_at, col_at, lat_tiles, lon_tiles):
    row_step = jnp.array([-1, -1, -1, 0, 0, 0, 1, 1, 1], dtype=jnp.int32)
    col_step = jnp.array([-1, 0, 1, -1, 0, 1, -1, 0, 1], dtype=jnp.int32)
    row_next = row_at + row_step
    across = (row_next < 0) | (row_next > lat_tiles - 1)
    col_next = (col_at + col_step + jnp.where(across, lon_tiles // 2, 0)) % lon_tiles
    row_next = jnp.clip(row_next, 0, lat_tiles - 1)
    return row_next * lon_tiles + col_next


def close_poles(rim_block, mirror):
    lat_index = lax.axis_index("lat")
    last_index = lax.axis_size("lat") - 1
    north_rim = jnp.where(lat_index == 0, mirror, rim_block[:1])
    south_rim = jnp.where(lat_index == last_index, mirror, rim_block[-1:])
    return jnp.concatenate([north_rim, rim_block[1:-1], south_rim], 0)


def around_pair(first_block, second_block):
    row_faces = (
        with_halo(first_block, (("lat", 0),), 1, False),
        with_halo(second_block, (("lat", 0),), 1, False),
    )
    mirror = passed_along((first_block, second_block), "lon", lax.axis_size("lon") // 2)
    column_a = close_poles(row_faces[0], mirror[0])
    column_b = close_poles(row_faces[1], mirror[1])
    return (
        with_halo(column_a, (("lon", 1),), 1, True),
        with_halo(column_b, (("lon", 1),), 1, True),
    )


def around_stats(log_total, out_dot):
    near_stats = (
        with_halo(log_total, (("lon", 1), ("lat", 0)), 1, True),
        with_halo(out_dot, (("lon", 1), ("lat", 0)), 1, True),
    )
    own_rows = log_total.shape[0]
    own_total = near_stats[0][1 : own_rows + 1]
    own_dot = near_stats[1][1 : own_rows + 1]
    mirror = passed_along((own_total, own_dot), "lon", lax.axis_size("lon") // 2)
    return (close_poles(near_stats[0], mirror[0]), close_poles(near_stats[1], mirror[1]))


def on_device(queries, key_tokens, value_tokens, out_grad, counts):
    own_rows = queries.shape[0]
    tile_len = queries.shape[2]
    feat_width = queries.shape[3]
    head_count = feat_width // HD
    lat_tiles = counts.shape[0]
    lon_tiles = counts.shape[1]
    row_base = lax.axis_index("lat") * own_rows
    col_at = lax.axis_index("lon")
    score_scale = 1.0 / math.sqrt(HD)
    positions = jnp.arange(tile_len, dtype=jnp.int32)
    flat_counts = counts.reshape(-1)
    near_k, near_v = around_pair(key_tokens, value_tokens)
    attended_rows, query_rows, total_rows, dot_rows = ([], [], [], [])
    row_local = 0
    slot_ids = neighbour_tiles(row_base + row_local, col_at, lat_tiles, lon_tiles)
    key_valid = (positions[None, :] < flat_counts[slot_ids][:, None]).reshape(-1)
    near_keys = near_k.reshape(9 * tile_len, feat_width)
    near_values = near_v.reshape(9 * tile_len, feat_width)
    head_outs = []
    query_parts = []
    head_totals = []
    head_dots = []
    for head_index in range(head_count):
        columns = slice(head_index * HD, (head_index + 1) * HD)
        query_here = queries[row_local, 0, :, columns]
        grad_here = out_grad[row_local, 0, :, columns]
        keys_head = near_keys[:, columns]
        values_head = near_values[:, columns]
        scores = (
            jnp.einsum("qd,kd->qk", query_here, keys_head, preferred_element_type=jnp.float32)
            * score_scale
        )
        row_max = jnp.max(jnp.where(key_valid[None, :], scores, -1e30), axis=-1, keepdims=True)
        row_total = jnp.sum(
            jnp.where(key_valid[None, :], jnp.exp(scores - row_max), 0.0), axis=-1, keepdims=True
        )
        log_total = row_max + jnp.log(row_total)
        weights = jnp.where(key_valid[None, :], jnp.exp(scores - log_total), 0.0)
        weights_low = weights.astype(jnp.bfloat16)
        head_out = jnp.dot(weights_low, values_head, preferred_element_type=jnp.float32).astype(
            jnp.bfloat16
        )
        out_dot = jnp.sum(grad_here.astype(jnp.float32) * head_out.astype(jnp.float32), axis=-1)
        grad_weights = jnp.einsum(
            "qd,kd->qk", grad_here, values_head, preferred_element_type=jnp.float32
        )
        grad_scores = (weights * (grad_weights - out_dot[:, None])).astype(jnp.bfloat16)
        query_part = (
            jnp.dot(grad_scores, keys_head, preferred_element_type=jnp.float32) * score_scale
        )
        head_outs.append(head_out)
        query_parts.append(query_part.astype(jnp.bfloat16))
        head_totals.append(log_total[:, 0])
        head_dots.append(out_dot)
    attended_rows.append(jnp.concatenate(head_outs, -1))
    query_rows.append(jnp.concatenate(query_parts, -1))
    total_rows.append(jnp.stack(head_totals))
    dot_rows.append(jnp.stack(head_dots))
    attended = jnp.stack(attended_rows)[:, None]
    query_grad = jnp.stack(query_rows)[:, None]
    own_totals = jnp.stack(total_rows)[:, None]
    own_dots = jnp.stack(dot_rows)[:, None]
    near_q, near_g = around_pair(queries, out_grad)
    near_total, near_dot = around_stats(own_totals, own_dots)
    key_rows, value_rows = ([], [])
    row_local = 0
    own_valid = positions < counts[row_base + row_local, col_at]
    near_queries = near_q.reshape(9 * tile_len, feat_width)
    near_grads = near_g.reshape(9 * tile_len, feat_width)
    key_parts = []
    value_parts = []
    for head_index in range(head_count):
        columns = slice(head_index * HD, (head_index + 1) * HD)
        queries_head = near_queries[:, columns]
        grads_head = near_grads[:, columns]
        keys_here = key_tokens[row_local, 0, :, columns]
        values_here = value_tokens[row_local, 0, :, columns]
        totals_head = near_total[:, :, head_index, :].reshape(9 * tile_len)
        dots_head = near_dot[:, :, head_index, :].reshape(9 * tile_len)
        scores = (
            jnp.einsum("qd,kd->qk", queries_head, keys_here, preferred_element_type=jnp.float32)
            * score_scale
        )
        weights = jnp.where(own_valid[None, :], jnp.exp(scores - totals_head[:, None]), 0.0)
        weights_low = weights.astype(jnp.bfloat16)
        value_part = jnp.einsum(
            "qk,qd->kd", weights_low, grads_head, preferred_element_type=jnp.float32
        )
        grad_weights = jnp.einsum(
            "qd,kd->qk", grads_head, values_here, preferred_element_type=jnp.float32
        )
        grad_scores = (weights * (grad_weights - dots_head[:, None])).astype(jnp.bfloat16)
        key_part = (
            jnp.einsum("qk,qd->kd", grad_scores, queries_head, preferred_element_type=jnp.float32)
            * score_scale
        )
        key_parts.append(key_part.astype(jnp.bfloat16))
        value_parts.append(value_part.astype(jnp.bfloat16))
    key_rows.append(jnp.concatenate(key_parts, -1))
    value_rows.append(jnp.concatenate(value_parts, -1))
    key_grad = jnp.stack(key_rows)[:, None]
    value_grad = jnp.stack(value_rows)[:, None]
    return (attended, query_grad, key_grad, value_grad)


def solution(mesh):
    placed = (
        P(("groups", "lat"), "lon", None, "head"),
        P(("groups", "lat"), "lon", None, "head"),
        P(("groups", "lat"), "lon", None, "head"),
        P(("groups", "lat"), "lon", None, "head"),
        P("groups", None),
    )
    return jax.shard_map(
        on_device,
        mesh=mesh,
        in_specs=placed,
        out_specs=(
            P(("groups", "lat"), "lon", None, "head"),
            P(("groups", "lat"), "lon", None, "head"),
            P(("groups", "lat"), "lon", None, "head"),
            P(("groups", "lat"), "lon", None, "head"),
        ),
        check_vma=False,
    )
```

profile of v0, /device:TPU:0, one launch (start us, length us, event | category | flops | bytes accessed | tf_op | source)
XLA Modules:
  0.0 219.1 jit_solution(3975038279234772611)
XLA Ops:
  0.7 4.1 %collective-permute-start.5 = (bf16[1,1,128,768]{3,2,1,0:T(8,128)(2,1)}, bf16[1,1,128,768]{3,2,1,0:T(8,128)(2,1)S(1)}, u32[]{:S(2)}, u32[]{:S(2)}) collective-permute-start(bf16[1,1,128,768]{3,2,1,0:T(8,128)(2,1)} %param.9), channel_id=1, source_target_pairs={{8,0},{12,4},{0,8},{4,12},{9,1},{13,5},{1,9},{5,13},{10,2},{14,6},... | collective-permute-start | bytes 589832 | tf_op jit(solution)/shard_map/ppermute | solution.py:31
  4.8 3.4 %collective-permute-start.6 = (bf16[1,1,128,768]{3,2,1,0:T(8,128)(2,1)}, bf16[1,1,128,768]{3,2,1,0:T(8,128)(2,1)S(1)}, u32[]{:S(2)}, u32[]{:S(2)}) collective-permute-start(bf16[1,1,128,768]{3,2,1,0:T(8,128)(2,1)} %param.9), channel_id=1, source_target_pairs={{0,2},{1,3},{4,6},{5,7},{8,10},{9,11},{12,14},{13,15},{16,18},{17,... | collective-permute-start | bytes 589832 | tf_op jit(solution)/shard_map/ppermute | solution.py:19
  8.2 1.3 collective-permute-start.7
  20.9 4.6 %collective-permute-start.1 = (bf16[1,1,128,768]{3,2,1,0:T(8,128)(2,1)}, bf16[1,1,128,768]{3,2,1,0:T(8,128)(2,1)S(1)}, u32[]{:S(2)}, u32[]{:S(2)}) collective-permute-start(bf16[1,1,128,768]{3,2,1,0:T(8,128)(2,1)} %param.8), channel_id=1, source_target_pairs={{0,2},{1,3},{4,6},{5,7},{8,10},{9,11},{12,14},{13,15},{16,18},{17,... | collective-permute-start | bytes 589832 | tf_op jit(solution)/shard_map/ppermute | solution.py:19
  25.6 2.7 %collective-permute-start.20 = (bf16[1,1,128,768]{3,2,1,0:T(8,128)(2,1)}, bf16[1,1,128,768]{3,2,1,0:T(8,128)(2,1)S(1)}, u32[]{:S(2)}, u32[]{:S(2)}) collective-permute-start(bf16[1,1,128,768]{3,2,1,0:T(8,128)(2,1)} %param.10), channel_id=1, source_target_pairs={{8,0},{12,4},{0,8},{4,12},{9,1},{13,5},{1,9},{5,13},{10,2},{14,6},... | collective-permute-start | bytes 589832 | tf_op jit(solution)/shard_map/ppermute | solution.py:31
  28.2 1.3 collective-permute-start.21
  29.5 1.3 collective-permute-start.22
  32.6 9.1 %collective-permute-done.20 = bf16[1,1,128,768]{3,2,1,0:T(8,128)(2,1)S(1)} collective-permute-done((bf16[1,1,128,768]{3,2,1,0:T(8,128)(2,1)}, bf16[1,1,128,768]{3,2,1,0:T(8,128)(2,1)S(1)}, u32[]{:S(2)}, u32[]{:S(2)}) %collective-permute-start.20) | collective-permute-done | bytes 196640 | tf_op jit(solution)/shard_map/ppermute | solution.py:31
  41.7 1.3 collective-permute-start.11
  43.1 2.7 %collective-permute-start.4 = (bf16[3,1,128,768]{3,2,1,0:T(8,128)(2,1)S(1)}, bf16[3,1,128,768]{3,2,1,0:T(8,128)(2,1)S(1)}, u32[]{:S(2)}, u32[]{:S(2)}) collective-permute-start(bf16[3,1,128,768]{3,2,1,0:T(8,128)(2,1)S(1)} %pad_maximum_fusion.4), channel_id=1, source_target_pairs={{4,0},{8,4},{12,8},{0,12},{5,1},{9,5},{13,9},{1,13},{6,2},{10,6},{... | collective-permute-start | bytes 1769480 | tf_op jit(solution)/shard_map/ppermute | solution.py:21
  46.0 3.9 %collective-permute-start.9 = (bf16[3,1,128,768]{3,2,1,0:T(8,128)(2,1)S(1)}, bf16[3,1,128,768]{3,2,1,0:T(8,128)(2,1)S(1)}, u32[]{:S(2)}, u32[]{:S(2)}) collective-permute-start(bf16[3,1,128,768]{3,2,1,0:T(8,128)(2,1)S(1)} %pad_maximum_fusion.5), channel_id=1, source_target_pairs={{4,0},{8,4},{12,8},{0,12},{5,1},{9,5},{13,9},{1,13},{6,2},{10,6},{... | collective-permute-start | bytes 1769480 | tf_op jit(solution)/shard_map/ppermute | solution.py:21
  51.0 3.8 %collective-permute-start.14 = (bf16[3,1,128,768]{3,2,1,0:T(8,128)(2,1)}, bf16[3,1,128,768]{3,2,1,0:T(8,128)(2,1)}, u32[]{:S(2)}, u32[]{:S(2)}) collective-permute-start(bf16[3,1,128,768]{3,2,1,0:T(8,128)(2,1)} %pad_maximum_fusion.6), channel_id=1, source_target_pairs={{4,0},{8,4},{12,8},{0,12},{5,1},{9,5},{13,9},{1,13},{6,2},{10,6},{... | collective-permute-start | bytes 1769480 | tf_op jit(solution)/shard_map/ppermute | solution.py:21
  55.7 15.7 %collective-permute-done.4 = bf16[3,1,128,768]{3,2,1,0:T(8,128)(2,1)S(1)} collective-permute-done((bf16[3,1,128,768]{3,2,1,0:T(8,128)(2,1)S(1)}, bf16[3,1,128,768]{3,2,1,0:T(8,128)(2,1)S(1)}, u32[]{:S(2)}, u32[]{:S(2)}) %collective-permute-start.4) | collective-permute-done | bytes 589856 | tf_op jit(solution)/shard_map/ppermute | solution.py:21
  71.4 1.3 collective-permute-done.3
  72.8 3.5 %collective-permute-start.24 = (bf16[3,1,128,768]{3,2,1,0:T(8,128)(2,1)}, bf16[3,1,128,768]{3,2,1,0:T(8,128)(2,1)}, u32[]{:S(2)}, u32[]{:S(2)}) collective-permute-start(bf16[3,1,128,768]{3,2,1,0:T(8,128)(2,1)} %pad_maximum_fusion.7), channel_id=1, source_target_pairs={{4,0},{8,4},{12,8},{0,12},{5,1},{9,5},{13,9},{1,13},{6,2},{10,6},{... | collective-permute-start | bytes 1769480 | tf_op jit(solution)/shard_map/ppermute | solution.py:21
  81.5 15.2 %collective-permute-done.9 = bf16[3,1,128,768]{3,2,1,0:T(8,128)(2,1)S(1)} collective-permute-done((bf16[3,1,128,768]{3,2,1,0:T(8,128)(2,1)S(1)}, bf16[3,1,128,768]{3,2,1,0:T(8,128)(2,1)S(1)}, u32[]{:S(2)}, u32[]{:S(2)}) %collective-permute-start.9) | collective-permute-done | bytes 589856 | tf_op jit(solution)/shard_map/ppermute | solution.py:21
  96.7 1.4 collective-permute-done.8
  100.7 2.1 fusion.89
  102.7 2.4 %constant_dynamic-update-slice_fusion.4 = (bf16[128,768]{0,1:T(8,128)(2,1)}, bf16[128,128]{0,1:T(8,128)(2,1)}) fusion(bf16[128,768]{0,1:T(8,128)(2,1)} %get-tuple-element.56, bf16[1152,768]{1,0:T(8,128)(2,1)} %bitcast.163, f32[1152,128]{1,0:T(8,128)} %copy-done.5, f32[128]{0:T(128)} %log_add_fusion.4, pred[1152]{0:T(1024)(128)(4,1)S(1)} %fusion.282), kind=kOutput, calls=%fused_computation.285 | convolution fusion | flops 38207488 | bytes 951936 | tf_op jit(solution)/shard_map/dot_general | solution.py:118
  105.1 2.3 %constant_dynamic-update-slice_fusion.3 = (bf16[128,768]{0,1:T(8,128)(2,1)}, bf16[128,128]{0,1:T(8,128)(2,1)}) fusion(bf16[128,768]{0,1:T(8,128)(2,1)} %get-tuple-element.58, bf16[1152,768]{1,0:T(8,128)(2,1)} %bitcast.164, f32[1152,128]{1,0:T(8,128)} %copy-done, f32[128]{0:T(128)} %log_add_fusion.3, pred[1152]{0:T(1024)(128)(4,1)S(1)} %fusion.282), kind=kOutput, calls=%fused_computation.284 | convolution fusion | flops 38207488 | bytes 951936 | tf_op jit(solution)/shard_map/dot_general | solution.py:118
  111.4 3.4 %collective-permute-start.16 = (f32[1,1,6,128]{3,2,1,0:T(8,128)S(1)}, f32[1,1,6,128]{3,2,1,0:T(8,128)S(1)}, u32[]{:S(2)}, u32[]{:S(2)}) collective-permute-start(f32[1,1,6,128]{3,2,1,0:T(8,128)S(1)} %bitcast.177), channel_id=1, source_target_pairs={{4,0},{8,4},{12,8},{0,12},{5,1},{9,5},{13,9},{1,13},{6,2},{10,6},{... | collective-permute-start | bytes 9224 | tf_op jit(solution)/shard_map/ppermute | solution.py:21
  115.6 2.3 %fusion.87 = bf16[128,768]{0,1:T(8,128)(2,1)} fusion(bf16[128,768]{0,1:T(8,128)(2,1)} %fusion.89, f32[1152,128]{1,0:T(8,128)} %copy-done.5, f32[128]{0:T(128)S(1)} %multiply_reduce_fusion.4, f32[128]{0:T(128)} %log_add_fusion.4, pred[1152]{0:T(1024)(128)(4,1)S(1)} %fusion.282, bf16[1152,768]{1,0:T(8,128)(2,1)} %bitcast.165, ...), kind=kOutput, calls=%fused_computation.116 | convolution fusion | flops 76267520 | bytes 1248256 | tf_op jit(solution)/shard_map/dot_general | solution.py:127
  117.9 1.3 multiply_reduce_fusion.3
  119.2 1.4 multiply_reduce_fusion.2
  120.6 1.3 multiply_reduce_fusion.1
  121.9 1.4 multiply_reduce_fusion
  124.0 2.1 fusion.85
  126.1 2.1 fusion.83
  128.3 3.8 %collective-permute-start.26 = (f32[1,1,6,128]{3,2,1,0:T(8,128)S(1)}, f32[1,1,6,128]{3,2,1,0:T(8,128)S(1)}, u32[]{:S(2)}, u32[]{:S(2)}) collective-permute-start(f32[1,1,6,128]{3,2,1,0:T(8,128)S(1)} %bitcast.182), channel_id=1, source_target_pairs={{4,0},{8,4},{12,8},{0,12},{5,1},{9,5},{13,9},{1,13},{6,2},{10,6},{... | collective-permute-start | bytes 9224 | tf_op jit(solution)/shard_map/ppermute | solution.py:21
  132.1 2.7 %pad_maximum_fusion.2 = bf16[3,3,128,768]{3,2,1,0:T(8,128)(2,1)} fusion(bf16[3,1,128,768]{3,2,1,0:T(8,128)(2,1)} %collective-permute-done.14, bf16[1,1,128,768]{3,2,1,0:T(8,128)(2,1)S(1)} %copy-done.16, bf16[1,1,128,768]{3,2,1,0:T(8,128)(2,1)S(1)} %copy-done.8, bf16[1,1,128,768]{3,2,1,0:T(8,128)(2,1)} %copy-done.17, ...), kind=kLoop, calls=%fused_computation.69 | loop fusion | flops 3538944 | bytes 3538944 | tf_op jit(solution)/shard_map/concatenate | solution.py:17
  134.8 2.2 fusion.81
  137.0 2.1 fusion.79
  139.1 8.6 %collective-permute-done.23 = bf16[3,1,128,768]{3,2,1,0:T(8,128)(2,1)} collective-permute-done((bf16[3,1,128,768]{3,2,1,0:T(8,128)(2,1)}, bf16[3,1,128,768]{3,2,1,0:T(8,128)(2,1)}, u32[]{:S(2)}, u32[]{:S(2)}) %collective-permute-start.23) | collective-permute-done | bytes 589856 | tf_op jit(solution)/shard_map/ppermute | solution.py:19
  147.7 1.4 pad_maximum_fusion.3
  149.2 1.9 copy.27
  151.0 1.7 copy.28
  154.3 2.0 collective-permute-start.19
  157.6 2.1 collective-permute-start.27
  159.8 2.0 collective-permute-start.29
  162.4 1.5 maximum_reduce_fusion.5
  163.9 1.3 sub.336
  166.5 1.5 maximum_reduce_fusion.4
  172.3 2.2 fusion.77
  175.8 1.9 fusion.21
  178.9 1.3 sub.348
  180.2 1.9 fusion.23
  182.1 1.3 sub.351
  183.4 1.5 fusion.284
  185.6 1.9 fusion.25
  187.5 1.5 fusion.283
  189.0 1.3 sub.357
  190.3 1.3 sub.360
  191.6 1.9 fusion.27
  193.5 1.3 sub.363
  195.4 1.9 fusion.29
  197.9 2.2 fusion.75
  200.0 2.2 fusion.73
  202.2 2.2 fusion.71
  204.4 2.2 fusion.69
  206.6 2.2 fusion.67
  208.7 1.8 copy.29
  210.6 2.0 fusion.94
  212.6 2.0 fusion.93
  217.4 1.7 copy.30
  (189 shorter events, 45.0 us)
Async XLA Ops:
  0.6 42.4 %copy-start.21 = (bf16[1,1,128,768]{3,2,1,0:T(8,128)(2,1)S(1)}, bf16[1,1,128,768]{3,2,1,0:T(8,128)(2,1)}, u32[]{:S(2)}) copy-start(bf16[1,1,128,768]{3,2,1,0:T(8,128)(2,1)} %param.8) | copy-start | bytes 589828
  0.6 41.1 %copy-start.6 = (bf16[1,1,128,768]{3,2,1,0:T(8,128)(2,1)S(1)}, bf16[1,1,128,768]{3,2,1,0:T(8,128)(2,1)}, u32[]{:S(2)}) copy-start(bf16[1,1,128,768]{3,2,1,0:T(8,128)(2,1)} %param.7) | copy-start | bytes 589828
  0.7 20.3 %collective-permute-start.5 = (bf16[1,1,128,768]{3,2,1,0:T(8,128)(2,1)}, bf16[1,1,128,768]{3,2,1,0:T(8,128)(2,1)S(1)}, u32[]{:S(2)}, u32[]{:S(2)}) collective-permute-start(bf16[1,1,128,768]{3,2,1,0:T(8,128)(2,1)} %param.9), channel_id=1, source_target_pairs={{8,0},{12,4},{0,8},{4,12},{9,1},{13,5},{1,9},{5,13},{10,2},{14,6},... | collective-permute-start | bytes 589832 | tf_op jit(solution)/shard_map/ppermute | solution.py:31
  4.8 20.8 %collective-permute-start.6 = (bf16[1,1,128,768]{3,2,1,0:T(8,128)(2,1)}, bf16[1,1,128,768]{3,2,1,0:T(8,128)(2,1)S(1)}, u32[]{:S(2)}, u32[]{:S(2)}) collective-permute-start(bf16[1,1,128,768]{3,2,1,0:T(8,128)(2,1)} %param.9), channel_id=1, source_target_pairs={{0,2},{1,3},{4,6},{5,7},{8,10},{9,11},{12,14},{13,15},{16,18},{17,... | collective-permute-start | bytes 589832 | tf_op jit(solution)/shard_map/ppermute | solution.py:19
  8.2 20.1 %collective-permute-start.7 = (bf16[1,1,128,768]{3,2,1,0:T(8,128)(2,1)}, bf16[1,1,128,768]{3,2,1,0:T(8,128)(2,1)S(1)}, u32[]{:S(2)}, u32[]{:S(2)}) collective-permute-start(bf16[1,1,128,768]{3,2,1,0:T(8,128)(2,1)} %param.9), channel_id=1, source_target_pairs={{2,0},{3,1},{6,4},{7,5},{10,8},{11,9},{14,12},{15,13},{18,16},{19,... | collective-permute-start | bytes 589832 | tf_op jit(solution)/shard_map/ppermute | solution.py:21
  9.5 20.1 %collective-permute-start = (bf16[1,1,128,768]{3,2,1,0:T(8,128)(2,1)}, bf16[1,1,128,768]{3,2,1,0:T(8,128)(2,1)S(1)}, u32[]{:S(2)}, u32[]{:S(2)}) collective-permute-start(bf16[1,1,128,768]{3,2,1,0:T(8,128)(2,1)} %param.8), channel_id=1, source_target_pairs={{8,0},{12,4},{0,8},{4,12},{9,1},{13,5},{1,9},{5,13},{10,2},{14,6},... | collective-permute-start | bytes 589832 | tf_op jit(solution)/shard_map/ppermute | solution.py:31
  9.9 21.0 %collective-permute-start.2 = (bf16[1,1,128,768]{3,2,1,0:T(8,128)(2,1)}, bf16[1,1,128,768]{3,2,1,0:T(8,128)(2,1)S(1)}, u32[]{:S(2)}, u32[]{:S(2)}) collective-permute-start(bf16[1,1,128,768]{3,2,1,0:T(8,128)(2,1)} %param.8), channel_id=1, source_target_pairs={{2,0},{3,1},{6,4},{7,5},{10,8},{11,9},{14,12},{15,13},{18,16},{19,... | collective-permute-start | bytes 589832 | tf_op jit(solution)/shard_map/ppermute | solution.py:21
  17.7 28.1 %copy-start.22 = (bf16[1,1,128,768]{3,2,1,0:T(8,128)(2,1)S(1)}, bf16[1,1,128,768]{3,2,1,0:T(8,128)(2,1)}, u32[]{:S(2)}) copy-start(bf16[1,1,128,768]{3,2,1,0:T(8,128)(2,1)} %param.9) | copy-start | bytes 589828
  20.9 10.3 %collective-permute-start.1 = (bf16[1,1,128,768]{3,2,1,0:T(8,128)(2,1)}, bf16[1,1,128,768]{3,2,1,0:T(8,128)(2,1)S(1)}, u32[]{:S(2)}, u32[]{:S(2)}) collective-permute-start(bf16[1,1,128,768]{3,2,1,0:T(8,128)(2,1)} %param.8), channel_id=1, source_target_pairs={{0,2},{1,3},{4,6},{5,7},{8,10},{9,11},{12,14},{13,15},{16,18},{17,... | collective-permute-start | bytes 589832 | tf_op jit(solution)/shard_map/ppermute | solution.py:19
  25.6 100.6 %copy-start.35 = (pred[1152]{0:T(1024)(128)(4,1)}, pred[1152]{0:T(1024)(128)(4,1)S(1)}, u32[]{:S(2)}) copy-start(pred[1152]{0:T(1024)(128)(4,1)S(1)} %fusion.282) | copy-start | bytes 3460
  25.6 16.1 %collective-permute-start.20 = (bf16[1,1,128,768]{3,2,1,0:T(8,128)(2,1)}, bf16[1,1,128,768]{3,2,1,0:T(8,128)(2,1)S(1)}, u32[]{:S(2)}, u32[]{:S(2)}) collective-permute-start(bf16[1,1,128,768]{3,2,1,0:T(8,128)(2,1)} %param.10), channel_id=1, source_target_pairs={{8,0},{12,4},{0,8},{4,12},{9,1},{13,5},{1,9},{5,13},{10,2},{14,6},... | collective-permute-start | bytes 589832 | tf_op jit(solution)/shard_map/ppermute | solution.py:31
  28.2 14.9 %collective-permute-start.21 = (bf16[1,1,128,768]{3,2,1,0:T(8,128)(2,1)}, bf16[1,1,128,768]{3,2,1,0:T(8,128)(2,1)S(1)}, u32[]{:S(2)}, u32[]{:S(2)}) collective-permute-start(bf16[1,1,128,768]{3,2,1,0:T(8,128)(2,1)} %param.10), channel_id=1, source_target_pairs={{0,2},{1,3},{4,6},{5,7},{8,10},{9,11},{12,14},{13,15},{16,18},{17,... | collective-permute-start | bytes 589832 | tf_op jit(solution)/shard_map/ppermute | solution.py:19
  29.5 16.3 %collective-permute-start.22 = (bf16[1,1,128,768]{3,2,1,0:T(8,128)(2,1)}, bf16[1,1,128,768]{3,2,1,0:T(8,128)(2,1)S(1)}, u32[]{:S(2)}, u32[]{:S(2)}) collective-permute-start(bf16[1,1,128,768]{3,2,1,0:T(8,128)(2,1)} %param.10), channel_id=1, source_target_pairs={{2,0},{3,1},{6,4},{7,5},{10,8},{11,9},{14,12},{15,13},{18,16},{19,... | collective-permute-start | bytes 589832 | tf_op jit(solution)/shard_map/ppermute | solution.py:21
  30.9 15.1 %collective-permute-start.10 = (bf16[1,1,128,768]{3,2,1,0:T(8,128)(2,1)}, bf16[1,1,128,768]{3,2,1,0:T(8,128)(2,1)S(1)}, u32[]{:S(2)}, u32[]{:S(2)}) collective-permute-start(bf16[1,1,128,768]{3,2,1,0:T(8,128)(2,1)} %param.7), channel_id=1, source_target_pairs={{8,0},{12,4},{0,8},{4,12},{9,1},{13,5},{1,9},{5,13},{10,2},{14,6},... | collective-permute-start | bytes 589832 | tf_op jit(solution)/shard_map/ppermute | solution.py:31
  31.3 18.6 %collective-permute-start.12 = (bf16[1,1,128,768]{3,2,1,0:T(8,128)(2,1)}, bf16[1,1,128,768]{3,2,1,0:T(8,128)(2,1)S(1)}, u32[]{:S(2)}, u32[]{:S(2)}) collective-permute-start(bf16[1,1,128,768]{3,2,1,0:T(8,128)(2,1)} %param.7), channel_id=1, source_target_pairs={{2,0},{3,1},{6,4},{7,5},{10,8},{11,9},{14,12},{15,13},{18,16},{19,... | collective-permute-start | bytes 589832 | tf_op jit(solution)/shard_map/ppermute | solution.py:21
  41.7 8.1 %collective-permute-start.11 = (bf16[1,1,128,768]{3,2,1,0:T(8,128)(2,1)S(1)}, bf16[1,1,128,768]{3,2,1,0:T(8,128)(2,1)S(1)}, u32[]{:S(2)}, u32[]{:S(2)}) collective-permute-start(bf16[1,1,128,768]{3,2,1,0:T(8,128)(2,1)S(1)} %copy-done.6), channel_id=1, source_target_pairs={{0,2},{1,3},{4,6},{5,7},{8,10},{9,11},{12,14},{13,15},{16,18},{17,... | collective-permute-start | bytes 589832 | tf_op jit(solution)/shard_map/ppermute | solution.py:19
  43.1 28.3 %collective-permute-start.4 = (bf16[3,1,128,768]{3,2,1,0:T(8,128)(2,1)S(1)}, bf16[3,1,128,768]{3,2,1,0:T(8,128)(2,1)S(1)}, u32[]{:S(2)}, u32[]{:S(2)}) collective-permute-start(bf16[3,1,128,768]{3,2,1,0:T(8,128)(2,1)S(1)} %pad_maximum_fusion.4), channel_id=1, source_target_pairs={{4,0},{8,4},{12,8},{0,12},{5,1},{9,5},{13,9},{1,13},{6,2},{10,6},{... | collective-permute-start | bytes 1769480 | tf_op jit(solution)/shard_map/ppermute | solution.py:21
  45.9 26.9 %collective-permute-start.3 = (bf16[3,1,128,768]{3,2,1,0:T(8,128)(2,1)S(1)}, bf16[3,1,128,768]{3,2,1,0:T(8,128)(2,1)S(1)}, u32[]{:S(2)}, u32[]{:S(2)}) collective-permute-start(bf16[3,1,128,768]{3,2,1,0:T(8,128)(2,1)S(1)} %pad_maximum_fusion.4), channel_id=1, source_target_pairs={{0,4},{4,8},{8,12},{12,0},{1,5},{5,9},{9,13},{13,1},{2,6},{6,10},{... | collective-permute-start | bytes 1769480 | tf_op jit(solution)/shard_map/ppermute | solution.py:19
  45.9 8.8 %copy-start.9 = (bf16[1,1,128,768]{3,2,1,0:T(8,128)(2,1)S(1)}, bf16[1,1,128,768]{3,2,1,0:T(8,128)(2,1)}, u32[]{:S(2)}) copy-start(bf16[1,1,128,768]{3,2,1,0:T(8,128)(2,1)} %param.10) | copy-start | bytes 589828
  46.0 50.7 %collective-permute-start.9 = (bf16[3,1,128,768]{3,2,1,0:T(8,128)(2,1)S(1)}, bf16[3,1,128,768]{3,2,1,0:T(8,128)(2,1)S(1)}, u32[]{:S(2)}, u32[]{:S(2)}) collective-permute-start(bf16[3,1,128,768]{3,2,1,0:T(8,128)(2,1)S(1)} %pad_maximum_fusion.5), channel_id=1, source_target_pairs={{4,0},{8,4},{12,8},{0,12},{5,1},{9,5},{13,9},{1,13},{6,2},{10,6},{... | collective-permute-start | bytes 1769480 | tf_op jit(solution)/shard_map/ppermute | solution.py:21
  49.8 48.2 %collective-permute-start.8 = (bf16[3,1,128,768]{3,2,1,0:T(8,128)(2,1)S(1)}, bf16[3,1,128,768]{3,2,1,0:T(8,128)(2,1)S(1)}, u32[]{:S(2)}, u32[]{:S(2)}) collective-permute-start(bf16[3,1,128,768]{3,2,1,0:T(8,128)(2,1)S(1)} %pad_maximum_fusion.5), channel_id=1, source_target_pairs={{0,4},{4,8},{8,12},{12,0},{1,5},{5,9},{9,13},{13,1},{2,6},{6,10},{... | collective-permute-start | bytes 1769480 | tf_op jit(solution)/shard_map/ppermute | solution.py:19
  49.9 22.8 %copy-start.11 = (bf16[1,1,128,768]{3,2,1,0:T(8,128)(2,1)}, bf16[1,1,128,768]{3,2,1,0:T(8,128)(2,1)S(1)}, u32[]{:S(2)}) copy-start(bf16[1,1,128,768]{3,2,1,0:T(8,128)(2,1)S(1)} %get-tuple-element.36) | copy-start | bytes 589828
  49.9 22.8 %copy-start.13 = (bf16[1,1,128,768]{3,2,1,0:T(8,128)(2,1)}, bf16[1,1,128,768]{3,2,1,0:T(8,128)(2,1)S(1)}, u32[]{:S(2)}) copy-start(bf16[1,1,128,768]{3,2,1,0:T(8,128)(2,1)S(1)} %get-tuple-element.37) | copy-start | bytes 589828
  49.9 22.8 %copy-start.15 = (bf16[1,1,128,768]{3,2,1,0:T(8,128)(2,1)}, bf16[1,1,128,768]{3,2,1,0:T(8,128)(2,1)S(1)}, u32[]{:S(2)}) copy-start(bf16[1,1,128,768]{3,2,1,0:T(8,128)(2,1)S(1)} %get-tuple-element.68) | copy-start | bytes 589828
  50.0 22.8 %copy-start.17 = (bf16[1,1,128,768]{3,2,1,0:T(8,128)(2,1)}, bf16[1,1,128,768]{3,2,1,0:T(8,128)(2,1)S(1)}, u32[]{:S(2)}) copy-start(bf16[1,1,128,768]{3,2,1,0:T(8,128)(2,1)S(1)} %get-tuple-element.69) | copy-start | bytes 589828
  51.0 77.3 %collective-permute-start.14 = (bf16[3,1,128,768]{3,2,1,0:T(8,128)(2,1)}, bf16[3,1,128,768]{3,2,1,0:T(8,128)(2,1)}, u32[]{:S(2)}, u32[]{:S(2)}) collective-permute-start(bf16[3,1,128,768]{3,2,1,0:T(8,128)(2,1)} %pad_maximum_fusion.6), channel_id=1, source_target_pairs={{4,0},{8,4},{12,8},{0,12},{5,1},{9,5},{13,9},{1,13},{6,2},{10,6},{... | collective-permute-start | bytes 1769480 | tf_op jit(solution)/shard_map/ppermute | solution.py:21
  71.4 56.9 %collective-permute-start.13 = (bf16[3,1,128,768]{3,2,1,0:T(8,128)(2,1)}, bf16[3,1,128,768]{3,2,1,0:T(8,128)(2,1)}, u32[]{:S(2)}, u32[]{:S(2)}) collective-permute-start(bf16[3,1,128,768]{3,2,1,0:T(8,128)(2,1)} %pad_maximum_fusion.6), channel_id=1, source_target_pairs={{0,4},{4,8},{8,12},{12,0},{1,5},{5,9},{9,13},{13,1},{2,6},{6,10},{... | collective-permute-start | bytes 1769480 | tf_op jit(solution)/shard_map/ppermute | solution.py:19
  72.8 66.3 %collective-permute-start.24 = (bf16[3,1,128,768]{3,2,1,0:T(8,128)(2,1)}, bf16[3,1,128,768]{3,2,1,0:T(8,128)(2,1)}, u32[]{:S(2)}, u32[]{:S(2)}) collective-permute-start(bf16[3,1,128,768]{3,2,1,0:T(8,128)(2,1)} %pad_maximum_fusion.7), channel_id=1, source_target_pairs={{4,0},{8,4},{12,8},{0,12},{5,1},{9,5},{13,9},{1,13},{6,2},{10,6},{... | collective-permute-start | bytes 1769480 | tf_op jit(solution)/shard_map/ppermute | solution.py:21
  78.8 19.3 %copy-start.23 = (bf16[1,1,128,768]{3,2,1,0:T(8,128)(2,1)S(1)}, bf16[1,1,128,768]{3,2,1,0:T(8,128)(2,1)}, u32[]{:S(2)}) copy-start(bf16[1,1,128,768]{3,2,1,0:T(8,128)(2,1)} %param.9) | copy-start | bytes 589828
  78.8 19.5 %copy-start.46 = (f32[128]{0:T(128)}, f32[128]{0:T(128)S(1)}, u32[]{:S(2)}) copy-start(f32[128]{0:T(128)S(1)} %log_add_fusion.5) | copy-start | bytes 1540
  81.4 27.1 %copy-start.43 = (f32[128]{0:T(128)}, f32[128]{0:T(128)S(1)}, u32[]{:S(2)}) copy-start(f32[128]{0:T(128)S(1)} %log_add_fusion.1) | copy-start | bytes 1540
  81.4 29.3 %copy-start.42 = (f32[128]{0:T(128)}, f32[128]{0:T(128)S(1)}, u32[]{:S(2)}) copy-start(f32[128]{0:T(128)S(1)} %log_add_fusion) | copy-start | bytes 1540
  81.4 19.2 %copy-start.28 = (bf16[1,1,128,128]{2,3,1,0:T(8,128)(2,1)S(1)}, bf16[1,1,128,128]{2,3,1,0:T(8,128)(2,1)}, u32[]{:S(2)}) copy-start(bf16[1,1,128,128]{2,3,1,0:T(8,128)(2,1)} %copy.31) | copy-start | bytes 98308
  96.7 51.0 %collective-permute-start.23 = (bf16[3,1,128,768]{3,2,1,0:T(8,128)(2,1)}, bf16[3,1,128,768]{3,2,1,0:T(8,128)(2,1)}, u32[]{:S(2)}, u32[]{:S(2)}) collective-permute-start(bf16[3,1,128,768]{3,2,1,0:T(8,128)(2,1)} %pad_maximum_fusion.7), channel_id=1, source_target_pairs={{0,4},{4,8},{8,12},{12,0},{1,5},{5,9},{9,13},{13,1},{2,6},{6,10},{... | collective-permute-start | bytes 1769480 | tf_op jit(solution)/shard_map/ppermute | solution.py:19
  100.7 6.8 %copy-start.40 = (f32[128]{0:T(128)}, f32[128]{0:T(128)S(1)}, u32[]{:S(2)}) copy-start(f32[128]{0:T(128)S(1)} %multiply_reduce_fusion.5) | copy-start | bytes 1540
  102.7 4.7 %copy-start.20 = (bf16[3,3,128,768]{3,2,1,0:T(8,128)(2,1)S(1)}, bf16[3,3,128,768]{3,2,1,0:T(8,128)(2,1)}, u32[]{:S(2)}) copy-start(bf16[3,3,128,768]{3,2,1,0:T(8,128)(2,1)} %copy-done.19) | copy-start | bytes 5308420
  102.7 4.7 %copy-start.44 = (f32[128]{0:T(128)S(1)}, f32[128]{0:T(128)}, u32[]{:S(2)}) copy-start(f32[128]{0:T(128)} %log_add_fusion.2) | copy-start | bytes 1540
  105.1 4.5 %copy-start.3 = (f32[1152,128]{1,0:T(8,128)S(1)}, f32[1152,128]{1,0:T(8,128)}, u32[]{:S(2)}) copy-start(f32[1152,128]{1,0:T(8,128)} %copy-done.2) | copy-start | bytes 1769476
  109.6 14.4 %copy-start.1 = (f32[1152,128]{1,0:T(8,128)S(1)}, f32[1152,128]{1,0:T(8,128)}, u32[]{:S(2)}) copy-start(f32[1152,128]{1,0:T(8,128)} %copy-done) | copy-start | bytes 1769476
  111.4 41.4 %collective-permute-start.16 = (f32[1,1,6,128]{3,2,1,0:T(8,128)S(1)}, f32[1,1,6,128]{3,2,1,0:T(8,128)S(1)}, u32[]{:S(2)}, u32[]{:S(2)}) collective-permute-start(f32[1,1,6,128]{3,2,1,0:T(8,128)S(1)} %bitcast.177), channel_id=1, source_target_pairs={{4,0},{8,4},{12,8},{0,12},{5,1},{9,5},{13,9},{1,13},{6,2},{10,6},{... | collective-permute-start | bytes 9224 | tf_op jit(solution)/shard_map/ppermute | solution.py:21
  115.6 7.7 %copy-start.41 = (f32[128]{0:T(128)}, f32[128]{0:T(128)S(1)}, u32[]{:S(2)}) copy-start(f32[128]{0:T(128)S(1)} %multiply_reduce_fusion.4) | copy-start | bytes 1540
  124.0 32.3 %copy-start.32 = (f32[6,128]{1,0:T(8,128)}, f32[6,128]{1,0:T(8,128)S(1)}, u32[]{:S(2)}) copy-start(f32[6,128]{1,0:T(8,128)S(1)} %stack.31) | copy-start | bytes 9220
  126.1 6.0 %copy-start.8 = (bf16[1,1,128,768]{3,2,1,0:T(8,128)(2,1)S(1)}, bf16[1,1,128,768]{3,2,1,0:T(8,128)(2,1)}, u32[]{:S(2)}) copy-start(bf16[1,1,128,768]{3,2,1,0:T(8,128)(2,1)} %param.7) | copy-start | bytes 589828
  126.1 6.0 %copy-start.16 = (bf16[1,1,128,768]{3,2,1,0:T(8,128)(2,1)S(1)}, bf16[1,1,128,768]{3,2,1,0:T(8,128)(2,1)}, u32[]{:S(2)}) copy-start(bf16[1,1,128,768]{3,2,1,0:T(8,128)(2,1)} %copy-done.15) | copy-start | bytes 589828
  128.3 24.5 %collective-permute-start.15 = (f32[1,1,6,128]{3,2,1,0:T(8,128)S(1)}, f32[1,1,6,128]{3,2,1,0:T(8,128)}, u32[]{:S(2)}, u32[]{:S(2)}) collective-permute-start(f32[1,1,6,128]{3,2,1,0:T(8,128)S(1)} %bitcast.178), channel_id=1, source_target_pairs={{0,4},{4,8},{8,12},{12,0},{1,5},{5,9},{9,13},{13,1},{2,6},{6,10},{... | collective-permute-start | bytes 9224 | tf_op jit(solution)/shard_map/ppermute | solution.py:19
  128.3 6.5 %copy-start.10 = (bf16[1,1,128,768]{3,2,1,0:T(8,128)(2,1)S(1)}, bf16[1,1,128,768]{3,2,1,0:T(8,128)(2,1)}, u32[]{:S(2)}) copy-start(bf16[1,1,128,768]{3,2,1,0:T(8,128)(2,1)} %param.10) | copy-start | bytes 589828
  128.3 28.0 %collective-permute-start.26 = (f32[1,1,6,128]{3,2,1,0:T(8,128)S(1)}, f32[1,1,6,128]{3,2,1,0:T(8,128)S(1)}, u32[]{:S(2)}, u32[]{:S(2)}) collective-permute-start(f32[1,1,6,128]{3,2,1,0:T(8,128)S(1)} %bitcast.182), channel_id=1, source_target_pairs={{4,0},{8,4},{12,8},{0,12},{5,1},{9,5},{13,9},{1,13},{6,2},{10,6},{... | collective-permute-start | bytes 9224 | tf_op jit(solution)/shard_map/ppermute | solution.py:21
  134.8 12.9 %copy-start.12 = (bf16[1,1,128,768]{3,2,1,0:T(8,128)(2,1)S(1)}, bf16[1,1,128,768]{3,2,1,0:T(8,128)(2,1)}, u32[]{:S(2)}) copy-start(bf16[1,1,128,768]{3,2,1,0:T(8,128)(2,1)} %copy-done.11) | copy-start | bytes 589828
  134.8 12.9 %copy-start.14 = (bf16[1,1,128,768]{3,2,1,0:T(8,128)(2,1)S(1)}, bf16[1,1,128,768]{3,2,1,0:T(8,128)(2,1)}, u32[]{:S(2)}) copy-start(bf16[1,1,128,768]{3,2,1,0:T(8,128)(2,1)} %copy-done.13) | copy-start | bytes 589828
  139.1 17.3 %collective-permute-start.25 = (f32[1,1,6,128]{3,2,1,0:T(8,128)S(1)}, f32[1,1,6,128]{3,2,1,0:T(8,128)}, u32[]{:S(2)}, u32[]{:S(2)}) collective-permute-start(f32[1,1,6,128]{3,2,1,0:T(8,128)S(1)} %bitcast.183), channel_id=1, source_target_pairs={{0,4},{4,8},{8,12},{12,0},{1,5},{5,9},{9,13},{13,1},{2,6},{6,10},{... | collective-permute-start | bytes 9224 | tf_op jit(solution)/shard_map/ppermute | solution.py:19
  149.2 23.2 %copy-start.18 = (bf16[3,3,128,768]{3,2,1,0:T(8,128)(2,1)S(1)}, bf16[3,3,128,768]{3,2,1,0:T(8,128)(2,1)}, u32[]{:S(2)}) copy-start(bf16[3,3,128,768]{3,2,1,0:T(8,128)(2,1)} %pad_maximum_fusion.2) | copy-start | bytes 5308420
  152.8 9.0 %copy-start.33 = (f32[1,1,6,128]{3,2,1,0:T(8,128)}, f32[1,1,6,128]{3,2,1,0:T(8,128)S(1)}, u32[]{:S(2)}) copy-start(f32[1,1,6,128]{3,2,1,0:T(8,128)S(1)} %collective-permute-done.16) | copy-start | bytes 9220
  153.5 6.3 %collective-permute-start.17 = (f32[1,3,6,128]{3,2,1,0:T(8,128)S(1)}, f32[1,3,6,128]{3,2,1,0:T(8,128)S(1)}, u32[]{:S(2)}, u32[]{:S(2)}) collective-permute-start(f32[1,3,6,128]{3,2,1,0:T(8,128)S(1)} %pad_maximum_fusion.8), channel_id=1, source_target_pairs={{8,0},{12,4},{0,8},{4,12},{9,1},{13,5},{1,9},{5,13},{10,2},{14,6},... | collective-permute-start | bytes 27656 | tf_op jit(solution)/shard_map/ppermute | solution.py:31
  154.3 7.5 %collective-permute-start.18 = (f32[1,3,6,128]{3,2,1,0:T(8,128)S(1)}, f32[1,3,6,128]{3,2,1,0:T(8,128)S(1)}, u32[]{:S(2)}, u32[]{:S(2)}) collective-permute-start(f32[1,3,6,128]{3,2,1,0:T(8,128)S(1)} %pad_maximum_fusion.8), channel_id=1, source_target_pairs={{0,2},{2,0},{1,3},{3,1},{4,6},{6,4},{5,7},{7,5},{8,10},{10,8},{9,1... | collective-permute-start | bytes 27656 | tf_op jit(solution)/shard_map/ppermute | solution.py:19
  154.3 7.5 %collective-permute-start.19 = (f32[1,3,6,128]{3,2,1,0:T(8,128)S(1)}, f32[1,3,6,128]{3,2,1,0:T(8,128)S(1)}, u32[]{:S(2)}, u32[]{:S(2)}) collective-permute-start(f32[1,3,6,128]{3,2,1,0:T(8,128)S(1)} %pad_maximum_fusion.8), channel_id=1, source_target_pairs={{2,0},{0,2},{3,1},{1,3},{6,4},{4,6},{7,5},{5,7},{10,8},{8,10},{11,... | collective-permute-start | bytes 27656 | tf_op jit(solution)/shard_map/ppermute | solution.py:21
  156.3 5.4 %copy-start.34 = (f32[1,1,6,128]{3,2,1,0:T(8,128)}, f32[1,1,6,128]{3,2,1,0:T(8,128)S(1)}, u32[]{:S(2)}) copy-start(f32[1,1,6,128]{3,2,1,0:T(8,128)S(1)} %collective-permute-done.26) | copy-start | bytes 9220
  157.6 7.5 %collective-permute-start.27 = (f32[1,3,6,128]{3,2,1,0:T(8,128)}, f32[1,3,6,128]{3,2,1,0:T(8,128)}, u32[]{:S(2)}, u32[]{:S(2)}) collective-permute-start(f32[1,3,6,128]{3,2,1,0:T(8,128)} %pad_maximum_fusion.9), channel_id=1, source_target_pairs={{8,0},{12,4},{0,8},{4,12},{9,1},{13,5},{1,9},{5,13},{10,2},{14,6},... | collective-permute-start | bytes 27656 | tf_op jit(solution)/shard_map/ppermute | solution.py:31
  159.7 5.4 %collective-permute-start.28 = (f32[1,3,6,128]{3,2,1,0:T(8,128)}, f32[1,3,6,128]{3,2,1,0:T(8,128)}, u32[]{:S(2)}, u32[]{:S(2)}) collective-permute-start(f32[1,3,6,128]{3,2,1,0:T(8,128)} %pad_maximum_fusion.9), channel_id=1, source_target_pairs={{0,2},{2,0},{1,3},{3,1},{4,6},{6,4},{5,7},{7,5},{8,10},{10,8},{9,1... | collective-permute-start | bytes 27656 | tf_op jit(solution)/shard_map/ppermute | solution.py:19
  159.8 5.4 %collective-permute-start.29 = (f32[1,3,6,128]{3,2,1,0:T(8,128)}, f32[1,3,6,128]{3,2,1,0:T(8,128)}, u32[]{:S(2)}, u32[]{:S(2)}) collective-permute-start(f32[1,3,6,128]{3,2,1,0:T(8,128)} %pad_maximum_fusion.9), channel_id=1, source_target_pairs={{2,0},{0,2},{3,1},{1,3},{6,4},{4,6},{7,5},{5,7},{10,8},{8,10},{11,... | collective-permute-start | bytes 27656 | tf_op jit(solution)/shard_map/ppermute | solution.py:21
  184.9 9.9 %copy-start.36 = (f32[3,3,128]{2,1,0:T(4,128)S(1)}, f32[3,3,128]{2,1,0:T(4,128)}, u32[]{:S(2)}) copy-start(f32[3,3,128]{2,1,0:T(4,128)} %get-tuple-element.15) | copy-start | bytes 13828
  195.4 4.7 %copy-start.37 = (f32[1152]{0:T(1024)S(1)}, f32[1152]{0:T(1024)}, u32[]{:S(2)}) copy-start(f32[1152]{0:T(1024)} %sub.351) | copy-start | bytes 13828
  208.7 5.9 %copy-start.24 = (f32[1152,128]{1,0:T(8,128)S(1)}, f32[1152,128]{1,0:T(8,128)}, u32[]{:S(2)}) copy-start(f32[1152,128]{1,0:T(8,128)} %fusion.25) | copy-start | bytes 1769476
  208.7 6.8 %copy-start.25 = (f32[1152,128]{1,0:T(8,128)S(1)}, f32[1152,128]{1,0:T(8,128)}, u32[]{:S(2)}) copy-start(f32[1152,128]{1,0:T(8,128)} %fusion.27) | copy-start | bytes 1769476
  210.6 5.9 %copy-start.26 = (f32[1152,128]{1,0:T(8,128)S(1)}, f32[1152,128]{1,0:T(8,128)}, u32[]{:S(2)}) copy-start(f32[1152,128]{1,0:T(8,128)} %fusion.29) | copy-start | bytes 1769476
  (13 other events, 24.0 us)
where the time goes:
time: 221 us; the launch traced here: 219 us
  matrix products  55 us (25%)
  waiting for transfers between devices  51.5 us (23%)
  starting transfers between devices  51.3 us (23%)
  local copies, waits for them, and re-layouts  34.2 us (15%)
  other arithmetic  25.9 us (12%)
    ppermute x12, waiting for transfers between devices, with_halo(): lax.ppermute(head, axis, [((i + 1) % count, i) for i in range(ends)])  31 us
    ppermute x12, starting transfers between devices, with_halo(): lax.ppermute(head, axis, [((i + 1) % count, i) for i in range(ends)])  30.2 us
    unnamed x104, local copies, waits for them, and re-layouts  15.7 us
    dot_general x6, matrix products, on_device(): jnp.einsum('qk,qd->kd', grad_scores, queries_head, preferred_element_type...  13 us
    dot_general x6, matrix products, on_device(): jnp.dot(grad_scores, keys_head, preferred_element_type=jnp.float32)  12.8 us
    ppermute x12, waiting for transfers between devices, with_halo(): lax.ppermute(tail, axis, [(i, (i + 1) % count) for i in range(ends)])  11.4 us
    dot_general x6, matrix products, on_device(): jnp.einsum('qd,kd->qk', queries_head, keys_here, preferred_element_type=j...  10.7 us
    ppermute x12, starting transfers between devices, with_halo(): lax.ppermute(tail, axis, [(i, (i + 1) % count) for i in range(ends)])  10.6 us
  transfers between devices with their start and end apart: 30, of which 6 were waited for; matrix products, arithmetic and copies ran while one was open for 27% of the time, Pallas kernels for 0%

commit v1 on v0

--- a/solution.py
+++ b/solution.py
@@ -3,9 +3,12 @@
 import jax
 import jax.numpy as jnp
 from jax import lax
+from jax.experimental import pallas as pl
+from jax.experimental.pallas import tpu as pltpu
 from jax.sharding import PartitionSpec as P
 
 HD = 128
+LOG2E = 1.4426950408889634
 
 
 def with_halo(cells, sides, width, closed):
@@ -75,7 +78,7 @@
     return (close_poles(near_stats[0], mirror[0]), close_poles(near_stats[1], mirror[1]))
 
 
-def on_device(queries, key_tokens, value_tokens, out_grad, counts):
+def on_device_general(queries, key_tokens, value_tokens, out_grad, counts):
     own_rows = queries.shape[0]
     tile_len = queries.shape[2]
     feat_width = queries.shape[3]
@@ -181,6 +184,235 @@
     return (attended, query_grad, key_grad, value_grad)
 
 
+TILES = 8
+COLS = 4
+HEADS_HERE = 6
+ARRAYS = 4
+
+
+def head_owner(head_index, core):
+    return jnp.where(core == 0, head_index + 1, head_index + 2 * (head_index // 3))
+
+
+def head_of(tile, core):
+    on_core0 = jnp.where((tile >= 1) & (tile <= 6), tile - 1, -1)
+    on_core1 = jnp.where(tile <= 2, tile, jnp.where(tile >= 5, tile - 2, -1))
+    return jnp.where(core == 0, on_core0, on_core1)
+
+
+def place(tile):
+    return {"lat": tile // COLS, "lon": tile % COLS}
+
+
+def head_kernel(
+    k_ref, v_ref, q_ref, g_ref, counts_ref,
+    out_ref, dq_ref, dk_ref, dv_ref,
+    got, made, key_sum, value_sum, bias_base,
+    in_send, in_recv, out_send, out_recv,
+):
+    scale = 1.0 / math.sqrt(HD)
+    lat = lax.axis_index("lat")
+    lon = lax.axis_index("lon")
+    core = lax.axis_index("head")
+    here = lat * COLS + lon
+    my_head = head_of(here, core)
+    works = my_head >= 0
+    sources = (k_ref, v_ref, q_ref, g_ref)
+    results = (out_ref, dq_ref, dk_ref, dv_ref)
+
+    barrier = pltpu.get_barrier_semaphore()
+    for step in range(1, TILES):
+        pl.semaphore_signal(
+            barrier, inc=1, device_id=place((here + step) % TILES),
+            device_id_type=pl.DeviceIdType.MESH,
+        )
+    pl.semaphore_wait(barrier, TILES - 1)
+
+    def send_in(array, head_index):
+        return pltpu.make_async_remote_copy(
+            src_ref=sources[array].at[0, 0, :, pl.ds(head_index * HD, HD)],
+            dst_ref=got.at[array, here],
+            send_sem=in_send.at[array, head_index],
+            recv_sem=in_recv.at[array, here],
+            device_id=place(head_owner(head_index, core)),
+            device_id_type=pl.DeviceIdType.MESH,
+        )
+
+    def keep_in(array, head_index):
+        return pltpu.make_async_copy(
+            sources[array].at[0, 0, :, pl.ds(head_index * HD, HD)],
+            got.at[array, here],
+            in_recv.at[array, here],
+        )
+
+    def send_out(array, tile):
+        columns = pl.ds(pl.multiple_of(my_head * HD, HD), HD)
+        return pltpu.make_async_remote_copy(
+            src_ref=made.at[array, tile],
+            dst_ref=results[array].at[0, 0, :, columns],
+            send_sem=out_send.at[array, tile],
+            recv_sem=out_recv.at[array, my_head],
+            device_id=place(tile),
+            device_id_type=pl.DeviceIdType.MESH,
+        )
+
+    def keep_out(array, tile):
+        columns = pl.ds(pl.multiple_of(my_head * HD, HD), HD)
+        return pltpu.make_async_copy(
+            made.at[array, tile],
+            results[array].at[0, 0, :, columns],
+            out_recv.at[array, my_head],
+        )
+
+    def start_out(array, tile):
+        @pl.when(tile != here)
+        def _():
+            send_out(array, tile).start()
+
+        @pl.when(tile == here)
+        def _():
+            keep_out(array, tile).start()
+
+    for array in range(ARRAYS):
+        for head_index in range(HEADS_HERE):
+            owner = head_owner(head_index, core)
+
+            @pl.when(owner != here)
+            def _():
+                send_in(array, head_index).start()
+
+            @pl.when(owner == here)
+            def _():
+                keep_in(array, head_index).start()
+
+    def await_in(array, tile):
+        pltpu.make_async_copy(
+            got.at[array, tile], got.at[array, tile], in_recv.at[array, tile]
+        ).wait()
+
+    @pl.when(works)
+    def _():
+        lanes = lax.broadcasted_iota(jnp.int32, (1, HD), 1)
+        for tile in range(TILES):
+            valid = lanes < counts_ref[tile // COLS, tile % COLS]
+            bias_base[:, tile * HD : (tile + 1) * HD] = jnp.where(valid, 0.0, -1e30)
+        key_sum[...] = jnp.zeros_like(key_sum)
+        value_sum[...] = jnp.zeros_like(value_sum)
+        for array in range(2):
+            for tile in range(TILES):
+                await_in(array, tile)
+        first_col = (lon // 2) * 2
+
+        def query_tile(step, carry):
+            row = step % 2
+            col = (first_col + step // 2) % COLS
+            tile = row * COLS + col
+            await_in(2, tile)
+            await_in(3, tile)
+            queries = got[2, tile]
+            grads = got[3, tile]
+            keys = got[0].reshape(TILES * HD, HD)
+            values = got[1].reshape(TILES * HD, HD)
+            key_tile = lax.broadcasted_iota(jnp.int32, (1, TILES * HD), 1) // HD
+            ahead = (key_tile % COLS - col + COLS) % COLS
+            times = jnp.where(
+                key_tile // COLS == row,
+                jnp.where(ahead % 2 == 1, 1.0, 0.0),
+                jnp.where(ahead == 2, -1e30, 0.0),
+            )
+            bias = bias_base[...] + times
+            scores = lax.dot_general(
+                queries, keys, (((1,), (1,)), ((), ())), preferred_element_type=jnp.float32
+            ) * (scale * LOG2E) + bias
+            row_max = jnp.max(scores, axis=-1, keepdims=True)
+            raised = jnp.exp2(scores - row_max)
+            row_total = jnp.sum(raised, axis=-1, keepdims=True)
+            weights = raised * (1.0 / row_total)
+            weights_low = weights.astype(jnp.bfloat16)
+            attended = jnp.dot(
+                weights_low, values, preferred_element_type=jnp.float32
+            ).astype(jnp.bfloat16)
+            made[0, tile] = attended
+            start_out(0, tile)
+            out_dot = jnp.sum(
+                grads.astype(jnp.float32) * attended.astype(jnp.float32), axis=-1, keepdims=True
+            )
+            grad_weights = lax.dot_general(
+                grads, values, (((1,), (1,)), ((), ())), preferred_element_type=jnp.float32
+            )
+            grad_scores = (weights * (grad_weights - out_dot)).astype(jnp.bfloat16)
+            made[1, tile] = (
+                jnp.dot(grad_scores, keys, preferred_element_type=jnp.float32) * scale
+            ).astype(jnp.bfloat16)
+            start_out(1, tile)
+            value_sum[...] += lax.dot_general(
+                grads, weights_low, (((0,), (0,)), ((), ())), preferred_element_type=jnp.float32
+            )
+            key_sum[...] += lax.dot_general(
+                queries, grad_scores, (((0,), (0,)), ((), ())), preferred_element_type=jnp.float32
+            )
+            return carry
+
+        lax.fori_loop(0, TILES, query_tile, 0)
+        for tile in range(TILES):
+            span = slice(tile * HD, (tile + 1) * HD)
+            made[2, tile] = (key_sum[:, span].T * scale).astype(jnp.bfloat16)
+            start_out(2, tile)
+            made[3, tile] = value_sum[:, span].T.astype(jnp.bfloat16)
+            start_out(3, tile)
+
+    for array in range(ARRAYS):
+        for head_index in range(HEADS_HERE):
+            @pl.when(head_owner(head_index, core) != here)
+            def _():
+                send_in(array, head_index).wait_send()
+
+    @pl.when(works)
+    def _():
+        for array in range(ARRAYS):
+            for tile in range(TILES):
+                @pl.when(here != tile)
+                def _():
+                    send_out(array, tile).wait_send()
+
+    for array in range(ARRAYS):
+        for head_index in range(HEADS_HERE):
+            block = results[array].at[0, 0, :, pl.ds(head_index * HD, HD)]
+            pltpu.make_async_copy(block, block, out_recv.at[array, head_index]).wait()
+
+
+def on_device_heads(queries, key_tokens, value_tokens, out_grad, counts):
+    shape = jax.ShapeDtypeStruct(queries.shape, queries.dtype)
+    anywhere = pl.BlockSpec(memory_space=pl.ANY)
+    return pl.pallas_call(
+        head_kernel,
+        out_shape=(shape,) * ARRAYS,
+        in_specs=[anywhere] * ARRAYS + [pl.BlockSpec(memory_space=pltpu.SMEM)],
+        out_specs=(anywhere,) * ARRAYS,
+        scratch_shapes=[
+            pltpu.VMEM((ARRAYS, TILES, HD, HD), jnp.bfloat16),
+            pltpu.VMEM((ARRAYS, TILES, HD, HD), jnp.bfloat16),
+            pltpu.VMEM((HD, TILES * HD), jnp.float32),
+            pltpu.VMEM((HD, TILES * HD), jnp.float32),
+            pltpu.VMEM((1, TILES * HD), jnp.float32),
+            pltpu.SemaphoreType.DMA((ARRAYS, HEADS_HERE)),
+            pltpu.SemaphoreType.DMA((ARRAYS, TILES)),
+            pltpu.SemaphoreType.DMA((ARRAYS, TILES)),
+            pltpu.SemaphoreType.DMA((ARRAYS, HEADS_HERE)),
+        ],
+        compiler_params=pltpu.CompilerParams(
+            collective_id=0, has_side_effects=True, vmem_limit_bytes=32 * 1024 * 1024
+        ),
+    )(key_tokens, value_tokens, queries, out_grad, counts)
+
+
+def on_device(queries, key_tokens, value_tokens, out_grad, counts):
+    rings = (lax.axis_size("lat"), lax.axis_size("lon"))
+    if rings == (TILES // COLS, COLS) and queries.shape == (1, 1, HD, HEADS_HERE * HD):
+        return on_device_heads(queries, key_tokens, value_tokens, out_grad, counts)
+    return on_device_general(queries, key_tokens, value_tokens, out_grad, counts)
+
+
 def solution(mesh):
     placed = (
         P(("groups", "lat"), "lon", None, "head"),

time: 221 us -> 50.4 us (0.23)
  the two profiles are of different devices: /device:TPU:0 before, /device:TPU:26 now
where the time goes in v1:
time: 50.4 us; the launch traced here: 50.2 us
  Pallas kernels  42.4 us (84%)
  local copies, waits for them, and re-layouts  7.09 us (14%)
  between operations  0.65 us (1%)
    pallas_call x1, Pallas kernels, on_device_heads(): pl.pallas_call(head_kernel, out_shape=(shape,) * ARRAYS, in_specs=[anywhe...  42.4 us
    unnamed x14, local copies, waits for them, and re-layouts  7.09 us

profile of v1, /device:TPU:26, one launch (start us, length us, event | category | flops | bytes accessed | tf_op | source)
XLA Modules:
  0.0 50.2 jit_solution(17450540056753363209)
XLA Ops:
  0.6 0.0 copy-start
  0.6 0.9 %copy-done = bf16[1,1,128,768]{3,2,1,0:T(8,128)(2,1)S(1)} copy-done((bf16[1,1,128,768]{3,2,1,0:T(8,128)(2,1)S(1)}, bf16[1,1,128,768]{3,2,1,0:T(8,128)(2,1)}, u32[]{:S(2)}) %copy-start) | copy-done | bytes 196632
  1.6 0.0 copy-start.1
  1.6 0.9 %copy-done.1 = bf16[1,1,128,768]{3,2,1,0:T(8,128)(2,1)S(1)} copy-done((bf16[1,1,128,768]{3,2,1,0:T(8,128)(2,1)S(1)}, bf16[1,1,128,768]{3,2,1,0:T(8,128)(2,1)}, u32[]{:S(2)}) %copy-start.1) | copy-done | bytes 196632
  2.5 0.0 copy-start.2
  2.5 0.9 %copy-done.2 = bf16[1,1,128,768]{3,2,1,0:T(8,128)(2,1)S(1)} copy-done((bf16[1,1,128,768]{3,2,1,0:T(8,128)(2,1)S(1)}, bf16[1,1,128,768]{3,2,1,0:T(8,128)(2,1)}, u32[]{:S(2)}) %copy-start.2) | copy-done | bytes 196632
  3.4 0.0 copy-start.3
  3.4 0.9 %copy-done.3 = bf16[1,1,128,768]{3,2,1,0:T(8,128)(2,1)S(1)} copy-done((bf16[1,1,128,768]{3,2,1,0:T(8,128)(2,1)S(1)}, bf16[1,1,128,768]{3,2,1,0:T(8,128)(2,1)}, u32[]{:S(2)}) %copy-start.3) | copy-done | bytes 196632
  4.3 0.0 copy-start.4
  4.3 0.7 %copy-done.4 = s32[2,4]{1,0:T(2,128)S(1)} copy-done((s32[2,4]{1,0:T(2,128)S(1)}, s32[2,4]{1,0:T(2,128)}, u32[]{:S(2)}) %copy-start.4) | copy-done | bytes 56
  5.0 42.4 %shard_map.84 = (bf16[1,1,128,768]{3,2,1,0:T(8,128)(2,1)S(1)}, bf16[1,1,128,768]{3,2,1,0:T(8,128)(2,1)S(1)}, bf16[1,1,128,768]{3,2,1,0:T(8,128)(2,1)S(1)}, bf16[1,1,128,768]{3,2,1,0:T(8,128)(2,1)S(1)}) custom-call(bf16[1,1,128,768]{3,2,1,0:T(8,128)(2,1)S(1)} %copy-done, bf16[1,1,128,768]{3,2,1,0:T(8,128)(2,1)S(1)} %copy-done.1, ...), custom_call_target="tpu_custom_call" | custom-call | tf_op jit(solution)/shard_map/pallas_call | solution.py:387
  47.5 0.7 %copy.13 = bf16[1,1,128,768]{3,2,1,0:T(8,128)(2,1)} copy(bf16[1,1,128,768]{3,2,1,0:T(8,128)(2,1)S(1)} %get-tuple-element.8) | data formatting | bytes 393216
  48.1 0.7 %copy.14 = bf16[1,1,128,768]{3,2,1,0:T(8,128)(2,1)} copy(bf16[1,1,128,768]{3,2,1,0:T(8,128)(2,1)S(1)} %get-tuple-element.9) | data formatting | bytes 393216
  48.8 0.7 %copy.15 = bf16[1,1,128,768]{3,2,1,0:T(8,128)(2,1)} copy(bf16[1,1,128,768]{3,2,1,0:T(8,128)(2,1)S(1)} %get-tuple-element.10) | data formatting | bytes 393216
  49.5 0.7 %copy.16 = bf16[1,1,128,768]{3,2,1,0:T(8,128)(2,1)} copy(bf16[1,1,128,768]{3,2,1,0:T(8,128)(2,1)S(1)} %get-tuple-element.11) | data formatting | bytes 393216
Async XLA Ops:
  0.6 0.9 %copy-start = (bf16[1,1,128,768]{3,2,1,0:T(8,128)(2,1)S(1)}, bf16[1,1,128,768]{3,2,1,0:T(8,128)(2,1)}, u32[]{:S(2)}) copy-start(bf16[1,1,128,768]{3,2,1,0:T(8,128)(2,1)} %k_ref.1) | copy-start | bytes 589828
  1.6 0.9 %copy-start.1 = (bf16[1,1,128,768]{3,2,1,0:T(8,128)(2,1)S(1)}, bf16[1,1,128,768]{3,2,1,0:T(8,128)(2,1)}, u32[]{:S(2)}) copy-start(bf16[1,1,128,768]{3,2,1,0:T(8,128)(2,1)} %v_ref.1) | copy-start | bytes 589828
  2.5 0.9 %copy-start.2 = (bf16[1,1,128,768]{3,2,1,0:T(8,128)(2,1)S(1)}, bf16[1,1,128,768]{3,2,1,0:T(8,128)(2,1)}, u32[]{:S(2)}) copy-start(bf16[1,1,128,768]{3,2,1,0:T(8,128)(2,1)} %q_ref.1) | copy-start | bytes 589828
  3.4 0.9 %copy-start.3 = (bf16[1,1,128,768]{3,2,1,0:T(8,128)(2,1)S(1)}, bf16[1,1,128,768]{3,2,1,0:T(8,128)(2,1)}, u32[]{:S(2)}) copy-start(bf16[1,1,128,768]{3,2,1,0:T(8,128)(2,1)} %g_ref.1) | copy-start | bytes 589828
  4.3 0.7 %copy-start.4 = (s32[2,4]{1,0:T(2,128)S(1)}, s32[2,4]{1,0:T(2,128)}, u32[]{:S(2)}) copy-start(s32[2,4]{1,0:T(2,128)} %counts_ref.1) | copy-start | bytes 100

commit v2 on v1

--- a/solution.py
+++ b/solution.py
@@ -208,7 +208,7 @@
     k_ref, v_ref, q_ref, g_ref, counts_ref,
     out_ref, dq_ref, dk_ref, dv_ref,
     got, made, key_sum, value_sum, bias_base,
-    in_send, in_recv, out_send, out_recv,
+    counts_here, staged, stage_sem, in_send, in_recv, out_send, out_recv, counts_sem,
 ):
     scale = 1.0 / math.sqrt(HD)
     lat = lax.axis_index("lat")
@@ -220,6 +220,14 @@
     sources = (k_ref, v_ref, q_ref, g_ref)
     results = (out_ref, dq_ref, dk_ref, dv_ref)
 
+    counts_copy = pltpu.make_async_copy(counts_ref, counts_here, counts_sem)
+    counts_copy.start()
+    stages = [
+        pltpu.make_async_copy(sources[array].at[0, 0], staged.at[array], stage_sem.at[array])
+        for array in range(ARRAYS)
+    ]
+    for stage in stages:
+        stage.start()
     barrier = pltpu.get_barrier_semaphore()
     for step in range(1, TILES):
         pl.semaphore_signal(
@@ -230,7 +238,7 @@
 
     def send_in(array, head_index):
         return pltpu.make_async_remote_copy(
-            src_ref=sources[array].at[0, 0, :, pl.ds(head_index * HD, HD)],
+            src_ref=staged.at[array, :, pl.ds(head_index * HD, HD)],
             dst_ref=got.at[array, here],
             send_sem=in_send.at[array, head_index],
             recv_sem=in_recv.at[array, here],
@@ -240,7 +248,7 @@
 
     def keep_in(array, head_index):
         return pltpu.make_async_copy(
-            sources[array].at[0, 0, :, pl.ds(head_index * HD, HD)],
+            staged.at[array, :, pl.ds(head_index * HD, HD)],
             got.at[array, here],
             in_recv.at[array, here],
         )
@@ -274,6 +282,7 @@
             keep_out(array, tile).start()
 
     for array in range(ARRAYS):
+        stages[array].wait()
         for head_index in range(HEADS_HERE):
             owner = head_owner(head_index, core)
 
@@ -290,11 +299,13 @@
             got.at[array, tile], got.at[array, tile], in_recv.at[array, tile]
         ).wait()
 
+    counts_copy.wait()
+
     @pl.when(works)
     def _():
         lanes = lax.broadcasted_iota(jnp.int32, (1, HD), 1)
         for tile in range(TILES):
-            valid = lanes < counts_ref[tile // COLS, tile % COLS]
+            valid = lanes < counts_here[tile // COLS, tile % COLS]
             bias_base[:, tile * HD : (tile + 1) * HD] = jnp.where(valid, 0.0, -1e30)
         key_sum[...] = jnp.zeros_like(key_sum)
         value_sum[...] = jnp.zeros_like(value_sum)
@@ -381,13 +392,18 @@
             pltpu.make_async_copy(block, block, out_recv.at[array, head_index]).wait()
 
 
+def hand_over(*refs):
+    for i in range(ARRAYS):
+        refs[ARRAYS + i][...] = refs[i][...]
+
+
 def on_device_heads(queries, key_tokens, value_tokens, out_grad, counts):
     shape = jax.ShapeDtypeStruct(queries.shape, queries.dtype)
     anywhere = pl.BlockSpec(memory_space=pl.ANY)
-    return pl.pallas_call(
+    results = pl.pallas_call(
         head_kernel,
         out_shape=(shape,) * ARRAYS,
-        in_specs=[anywhere] * ARRAYS + [pl.BlockSpec(memory_space=pltpu.SMEM)],
+        in_specs=[pl.BlockSpec(memory_space=pltpu.HBM)] * (ARRAYS + 1),
         out_specs=(anywhere,) * ARRAYS,
         scratch_shapes=[
             pltpu.VMEM((ARRAYS, TILES, HD, HD), jnp.bfloat16),
@@ -395,15 +411,27 @@
             pltpu.VMEM((HD, TILES * HD), jnp.float32),
             pltpu.VMEM((HD, TILES * HD), jnp.float32),
             pltpu.VMEM((1, TILES * HD), jnp.float32),
+            pltpu.SMEM(counts.shape, jnp.int32),
+            pltpu.VMEM((ARRAYS, HD, HEADS_HERE * HD), jnp.bfloat16),
+            pltpu.SemaphoreType.DMA((ARRAYS,)),
             pltpu.SemaphoreType.DMA((ARRAYS, HEADS_HERE)),
             pltpu.SemaphoreType.DMA((ARRAYS, TILES)),
             pltpu.SemaphoreType.DMA((ARRAYS, TILES)),
             pltpu.SemaphoreType.DMA((ARRAYS, HEADS_HERE)),
+            pltpu.SemaphoreType.DMA,
         ],
         compiler_params=pltpu.CompilerParams(
-            collective_id=0, has_side_effects=True, vmem_limit_bytes=32 * 1024 * 1024
+            collective_id=0, has_side_effects=True, vmem_limit_bytes=62 * 1024 * 1024
         ),
     )(key_tokens, value_tokens, queries, out_grad, counts)
+    return pl.pallas_call(
+        hand_over,
+        out_shape=(shape,) * ARRAYS,
+        in_specs=[pl.BlockSpec(memory_space=pltpu.VMEM)] * ARRAYS,
+        out_specs=(pl.BlockSpec(memory_space=pltpu.VMEM),) * ARRAYS,
+        scratch_shapes=[],
+        compiler_params=pltpu.CompilerParams(vmem_limit_bytes=62 * 1024 * 1024),
+    )(*results)
 
 
 def on_device(queries, key_tokens, value_tokens, out_grad, counts):

time: 50.4 us -> 44.9 us (0.89)
  local copies, waits for them, and re-layouts: 7.09 us -> 0 us
  Pallas kernels: 42.4 us -> 44.1 us
    unnamed x14 -> x0, local copies, waits for them, and re-layouts: 7.09 us -> none
    pallas_call x1 -> x2, Pallas kernels: 42.4 us -> 44.1 us  [the longest x1 42 us: on_device_heads(): pl.pallas_call(head_kernel, out_shape=(shape,) * ARRAYS, in_specs=[pl.Blo...]
where the time goes in v2:
time: 44.9 us; the launch traced here: 44.8 us
  Pallas kernels  44.1 us (98%)
  between operations  0.64 us (1%)
    pallas_call x1, Pallas kernels, on_device_heads(): pl.pallas_call(head_kernel, out_shape=(shape,) * ARRAYS, in_specs=[pl.Blo...  42 us
    pallas_call x1, Pallas kernels, on_device_heads(): pl.pallas_call(hand_over, out_shape=(shape,) * ARRAYS, in_specs=[pl.Block...  2.11 us

profile of v2, /device:TPU:26, one launch (start us, length us, event | category | flops | bytes accessed | tf_op | source)
XLA Modules:
  0.0 44.8 jit_solution(6719968706151971539)
XLA Ops:
  0.6 42.0 %shard_map.84 = (bf16[1,1,128,768]{3,2,1,0:T(8,128)(2,1)}, bf16[1,1,128,768]{3,2,1,0:T(8,128)(2,1)}, bf16[1,1,128,768]{3,2,1,0:T(8,128)(2,1)}, bf16[1,1,128,768]{3,2,1,0:T(8,128)(2,1)}) custom-call(bf16[1,1,128,768]{3,2,1,0:T(8,128)(2,1)} %k_ref.1, bf16[1,1,128,768]{3,2,1,0:T(8,128)(2,1)} %v_ref.1, bf16[1,1,128,768]{3,2,1,0:T(8,128)(2,1)} %q_ref.1, ...), custom_call_target="tpu_custom_call" | custom-call | tf_op jit(solution)/shard_map/pallas_call | solution.py:403
  42.7 2.1 %shard_map.85 = (bf16[1,1,128,768]{3,2,1,0:T(8,128)(2,1)}, bf16[1,1,128,768]{3,2,1,0:T(8,128)(2,1)}, bf16[1,1,128,768]{3,2,1,0:T(8,128)(2,1)}, bf16[1,1,128,768]{3,2,1,0:T(8,128)(2,1)}) custom-call(bf16[1,1,128,768]{3,2,1,0:T(8,128)(2,1)} %get-tuple-element.8.refs_0_, bf16[1,1,128,768]{3,2,1,0:T(8,128)(2,1)} %get-tuple-element.9.refs_1_, ...), custom_call_target="tpu_custom_call" | custom-call | tf_op jit(solution)/shard_map/pallas_call | solution.py:427

commit v3 on v2

--- a/solution.py
+++ b/solution.py
@@ -208,7 +208,7 @@
     k_ref, v_ref, q_ref, g_ref, counts_ref,
     out_ref, dq_ref, dk_ref, dv_ref,
     got, made, key_sum, value_sum, bias_base,
-    counts_here, staged, stage_sem, in_send, in_recv, out_send, out_recv, counts_sem,
+    kept, counts_here, staged, stage_sem, in_send, in_recv, out_send, out_recv, counts_sem,
 ):
     scale = 1.0 / math.sqrt(HD)
     lat = lax.axis_index("lat")
@@ -319,9 +319,7 @@
             col = (first_col + step // 2) % COLS
             tile = row * COLS + col
             await_in(2, tile)
-            await_in(3, tile)
             queries = got[2, tile]
-            grads = got[3, tile]
             keys = got[0].reshape(TILES * HD, HD)
             values = got[1].reshape(TILES * HD, HD)
             key_tile = lax.broadcasted_iota(jnp.int32, (1, TILES * HD), 1) // HD
@@ -343,8 +341,23 @@
             attended = jnp.dot(
                 weights_low, values, preferred_element_type=jnp.float32
             ).astype(jnp.bfloat16)
+            kept[tile] = weights
             made[0, tile] = attended
             start_out(0, tile)
+            return carry
+
+        def query_tile_back(step, carry):
+            row = step % 2
+            col = (first_col + step // 2) % COLS
+            tile = row * COLS + col
+            await_in(3, tile)
+            queries = got[2, tile]
+            grads = got[3, tile]
+            keys = got[0].reshape(TILES * HD, HD)
+            values = got[1].reshape(TILES * HD, HD)
+            weights = kept[tile]
+            weights_low = weights.astype(jnp.bfloat16)
+            attended = made[0, tile]
             out_dot = jnp.sum(
                 grads.astype(jnp.float32) * attended.astype(jnp.float32), axis=-1, keepdims=True
             )
@@ -365,6 +378,7 @@
             return carry
 
         lax.fori_loop(0, TILES, query_tile, 0)
+        lax.fori_loop(0, TILES, query_tile_back, 0)
         for tile in range(TILES):
             span = slice(tile * HD, (tile + 1) * HD)
             made[2, tile] = (key_sum[:, span].T * scale).astype(jnp.bfloat16)
@@ -411,6 +425,7 @@
             pltpu.VMEM((HD, TILES * HD), jnp.float32),
             pltpu.VMEM((HD, TILES * HD), jnp.float32),
             pltpu.VMEM((1, TILES * HD), jnp.float32),
+            pltpu.VMEM((TILES, HD, TILES * HD), jnp.float32),
             pltpu.SMEM(counts.shape, jnp.int32),
             pltpu.VMEM((ARRAYS, HD, HEADS_HERE * HD), jnp.bfloat16),
             pltpu.SemaphoreType.DMA((ARRAYS,)),

time: 44.9 us -> 43.3 us (0.964)
  Pallas kernels: 44.1 us -> 42.5 us
    pallas_call x1, Pallas kernels: 42 us -> 40.4 us  [on_device_heads(): pl.pallas_call(head_kernel, out_shape=(shape,) * ARRAYS, in_specs=[pl.Blo...]
where the time goes in v3:
time: 43.3 us; the launch traced here: 43.1 us
  Pallas kernels  42.5 us (98%)
  between operations  0.64 us (1%)
    pallas_call x1, Pallas kernels, on_device_heads(): pl.pallas_call(head_kernel, out_shape=(shape,) * ARRAYS, in_specs=[pl.Blo...  40.4 us
    pallas_call x1, Pallas kernels, on_device_heads(): pl.pallas_call(hand_over, out_shape=(shape,) * ARRAYS, in_specs=[pl.Block...  2.11 us

profile of v3, /device:TPU:26, one launch (start us, length us, event | category | flops | bytes accessed | tf_op | source)
XLA Modules:
  0.0 43.1 jit_solution(3198815696659317988)
XLA Ops:
  0.6 40.4 %shard_map.84 = (bf16[1,1,128,768]{3,2,1,0:T(8,128)(2,1)}, bf16[1,1,128,768]{3,2,1,0:T(8,128)(2,1)}, bf16[1,1,128,768]{3,2,1,0:T(8,128)(2,1)}, bf16[1,1,128,768]{3,2,1,0:T(8,128)(2,1)}) custom-call(bf16[1,1,128,768]{3,2,1,0:T(8,128)(2,1)} %k_ref.1, bf16[1,1,128,768]{3,2,1,0:T(8,128)(2,1)} %v_ref.1, bf16[1,1,128,768]{3,2,1,0:T(8,128)(2,1)} %q_ref.1, ...), custom_call_target="tpu_custom_call" | custom-call | tf_op jit(solution)/shard_map/pallas_call | solution.py:417
  41.0 2.1 %shard_map.85 = (bf16[1,1,128,768]{3,2,1,0:T(8,128)(2,1)}, bf16[1,1,128,768]{3,2,1,0:T(8,128)(2,1)}, bf16[1,1,128,768]{3,2,1,0:T(8,128)(2,1)}, bf16[1,1,128,768]{3,2,1,0:T(8,128)(2,1)}) custom-call(bf16[1,1,128,768]{3,2,1,0:T(8,128)(2,1)} %get-tuple-element.8.refs_0_, bf16[1,1,128,768]{3,2,1,0:T(8,128)(2,1)} %get-tuple-element.9.refs_1_, ...), custom_call_target="tpu_custom_call" | custom-call | tf_op jit(solution)/shard_map/pallas_call | solution.py:442

commit v4 on v3

--- a/solution.py
+++ b/solution.py
@@ -377,8 +377,8 @@
             )
             return carry
 
-        lax.fori_loop(0, TILES, query_tile, 0)
-        lax.fori_loop(0, TILES, query_tile_back, 0)
+        lax.fori_loop(0, TILES, query_tile, 0, unroll=2)
+        lax.fori_loop(0, TILES, query_tile_back, 0, unroll=2)
         for tile in range(TILES):
             span = slice(tile * HD, (tile + 1) * HD)
             made[2, tile] = (key_sum[:, span].T * scale).astype(jnp.bfloat16)
@@ -407,8 +407,18 @@
 
 
 def hand_over(*refs):
-    for i in range(ARRAYS):
-        refs[ARRAYS + i][...] = refs[i][...]
+    halves, sems = refs[2 * ARRAYS], refs[2 * ARRAYS + 1]
+    loads = [pltpu.make_async_copy(refs[i], halves.at[i], sems.at[0, i]) for i in range(ARRAYS)]
+    saves = [
+        pltpu.make_async_copy(halves.at[i], refs[ARRAYS + i], sems.at[1, i]) for i in range(ARRAYS)
+    ]
+    for load in loads:
+        load.start()
+    for load, save in zip(loads, saves):
+        load.wait()
+        save.start()
+    for save in saves:
+        save.wait()
 
 
 def on_device_heads(queries, key_tokens, value_tokens, out_grad, counts):
@@ -442,9 +452,9 @@
     return pl.pallas_call(
         hand_over,
         out_shape=(shape,) * ARRAYS,
-        in_specs=[pl.BlockSpec(memory_space=pltpu.VMEM)] * ARRAYS,
-        out_specs=(pl.BlockSpec(memory_space=pltpu.VMEM),) * ARRAYS,
-        scratch_shapes=[],
+        in_specs=[pl.BlockSpec(memory_space=pltpu.HBM)] * ARRAYS,
+        out_specs=(pl.BlockSpec(memory_space=pltpu.HBM),) * ARRAYS,
+        scratch_shapes=[pltpu.VMEM((ARRAYS,) + queries.shape, queries.dtype), pltpu.SemaphoreType.DMA((2, ARRAYS))],
         compiler_params=pltpu.CompilerParams(vmem_limit_bytes=62 * 1024 * 1024),
     )(*results)
 

time: 43.3 us -> 42.8 us (0.988)
  Pallas kernels: 42.5 us -> 42 us
where the time goes in v4:
time: 42.8 us; the launch traced here: 42.7 us
  Pallas kernels  42 us (98%)
  between operations  0.64 us (1%)
    pallas_call x1, Pallas kernels, on_device_heads(): pl.pallas_call(head_kernel, out_shape=(shape,) * ARRAYS, in_specs=[pl.Blo...  40.1 us
    pallas_call x1, Pallas kernels, on_device_heads(): pl.pallas_call(hand_over, out_shape=(shape,) * ARRAYS, in_specs=[pl.Block...  1.97 us

profile of v4, /device:TPU:26, one launch (start us, length us, event | category | flops | bytes accessed | tf_op | source)
XLA Modules:
  0.0 42.7 jit_solution(14645456114515102780)
XLA Ops:
  0.6 40.1 %shard_map.84 = (bf16[1,1,128,768]{3,2,1,0:T(8,128)(2,1)}, bf16[1,1,128,768]{3,2,1,0:T(8,128)(2,1)}, bf16[1,1,128,768]{3,2,1,0:T(8,128)(2,1)}, bf16[1,1,128,768]{3,2,1,0:T(8,128)(2,1)}) custom-call(bf16[1,1,128,768]{3,2,1,0:T(8,128)(2,1)} %k_ref.1, bf16[1,1,128,768]{3,2,1,0:T(8,128)(2,1)} %v_ref.1, bf16[1,1,128,768]{3,2,1,0:T(8,128)(2,1)} %q_ref.1, ...), custom_call_target="tpu_custom_call" | custom-call | tf_op jit(solution)/shard_map/pallas_call | solution.py:427
  40.7 2.0 %shard_map.85 = (bf16[1,1,128,768]{3,2,1,0:T(8,128)(2,1)}, bf16[1,1,128,768]{3,2,1,0:T(8,128)(2,1)}, bf16[1,1,128,768]{3,2,1,0:T(8,128)(2,1)}, bf16[1,1,128,768]{3,2,1,0:T(8,128)(2,1)}) custom-call(bf16[1,1,128,768]{3,2,1,0:T(8,128)(2,1)} %get-tuple-element.8.refs_0_, bf16[1,1,128,768]{3,2,1,0:T(8,128)(2,1)} %get-tuple-element.9.refs_1_, ...), custom_call_target="tpu_custom_call" | custom-call | tf_op jit(solution)/shard_map/pallas_call | solution.py:452
